TPU v7x, 32 devices: a whole 2x2x4 slice. The times are simulated.
32 devices in a mesh: blk: 8 (over z, x), tile: 4 (over y, core).
Axes of the slice: x: 2, y: 2, z: 4, core: 2. Of those that a mesh axis runs over, the one named last changes fastest.
Arguments:
- stream_in: bfloat16 [32, 16, 16, 2240], P('tile', 'blk'), may hold values from -6 to 6
- queries: bfloat16 [32, 16, 16, 2240], P('tile', 'blk'), may hold values from -12 to 12
- key_rows: bfloat16 [32, 16, 16, 2240], P('tile', 'blk'), may hold values from -12 to 12
- value_rows: bfloat16 [32, 16, 16, 2240], P('tile', 'blk'), may hold values from -12 to 12
- w_output: bfloat16 [2240, 2240], P('tile'), may hold values from -0.125 to 0.125
- w_inner: bfloat16 [2240, 2, 4096], P(None, None, 'tile'), may hold values from -0.125 to 0.125
- w_down: bfloat16 [4096, 2240], P('tile'), may hold values from -0.09375 to 0.09375
- spatial_taps: float32 [3, 3, 2, 4096], P(None, None, None, 'tile'), may hold values from -2 to 2
- temporal_taps: float32 [3, 2, 4096], P(None, None, 'tile'), may hold values from -3.5 to 3.5
Outputs:
- layer_out: bfloat16 [32, 16, 16, 2240], P('tile', 'blk')
All inputs are finite; a program needn't handle non-finite values.
Results may differ from a plain program's by a relative error of at most 0.009.
Values may be sent and summed in bfloat16 or wider, within the bound.
A program may use at most 128 MiB of HBM per device.

v0:
```python
import jax
import jax.numpy as jnp
from jax import lax
from jax.sharding import PartitionSpec as P

HEADS = 20
HEAD_DIM = 112
TAPS = 3
EPS = 1e-06


def from_partner(value, axis, stride):
    mask = 2**stride
    pairs = [(source, source ^ mask) for source in range(lax.axis_size(axis))]
    return lax.ppermute(value, axis, pairs)


def carried_in(x, axis, combine, identity):
    peers, position = (lax.axis_size(axis), lax.axis_index(axis))
    everything = jax.tree.map(lambda part: lax.all_gather(part, axis), x)
    start = jax.tree.map(
        lambda part, zero: jnp.broadcast_to(jnp.asarray(zero, part.dtype), part.shape), x, identity
    )

    def step(k, before):
        reached = k < position
        new = combine(before, jax.tree.map(lambda part: part[k], everything))
        return jax.tree.map(lambda a, b: jnp.where(reached, a, b), new, before)

    return lax.fori_loop(0, peers, step, start)


def shifted(x, axis, by):
    peers = lax.axis_size(axis)
    pairs = [(i, i + by) for i in range(peers) if 0 <= i + by < peers]
    return lax.ppermute(x, axis, pairs)


def add_pair(earlier, later):
    return (earlier[0] + later[0], earlier[1] + later[1])


def prefix_state(state_parts):
    partner = from_partner((state_parts[0], state_parts[1]), "blk", 0)
    block_sum = add_pair(state_parts, partner)
    odd_side = (lax.axis_index("blk") % 2).astype(jnp.float32)
    keep_share = 1.0 - 0.5 * odd_side
    zero_state = (jnp.zeros_like(block_sum[0]), jnp.zeros_like(block_sum[1]))
    before = carried_in((block_sum[0] * 0.5, block_sum[1] * 0.5), "blk", add_pair, zero_state)
    return (before[0] + block_sum[0] * keep_share, before[1] + block_sum[1] * keep_share)


def spatial_conv(inner_act, spatial_taps):
    row_count = inner_act.shape[0]
    col_count = inner_act.shape[2]
    padded = jnp.pad(inner_act, ((1, 1), (0, 0), (1, 1), (0, 0), (0, 0)))
    running = jnp.zeros(inner_act.shape, jnp.float32)
    for tap_row in range(3):
        for tap_col in range(3):
            window = padded[tap_row : tap_row + row_count, :, tap_col : tap_col + col_count]
            running = running + window.astype(jnp.float32) * spatial_taps[tap_row, tap_col]
    return running


def on_device(
    stream_in, queries, key_rows, value_rows, w_output, w_inner, w_down, spatial_taps, temporal_taps
):
    row_count, frames, col_count, model_width = queries.shape
    tokens = row_count * frames * col_count
    highest = lax.Precision.HIGHEST
    key_pos = jax.nn.relu(key_rows).reshape(tokens, HEADS, HEAD_DIM)
    value_heads = value_rows.reshape(tokens, HEADS, HEAD_DIM)
    local_kv = jnp.einsum("thd,the->hde", key_pos, value_heads, preferred_element_type=jnp.float32)
    local_kv = local_kv.reshape(model_width, HEAD_DIM)
    local_z = jnp.sum(key_pos.astype(jnp.float32), axis=0).reshape(model_width)
    shares = (
        lax.psum_scatter(local_kv, "tile", scatter_dimension=0, tiled=True),
        lax.psum_scatter(local_z, "tile", scatter_dimension=0, tiled=True),
    )
    share_state = prefix_state(shares)
    state, zsum = (
        lax.all_gather(share_state[0], "tile", axis=0, tiled=True),
        lax.all_gather(share_state[1], "tile", axis=0, tiled=True),
    )
    state = state.reshape(HEADS, HEAD_DIM, HEAD_DIM)
    zsum = zsum.reshape(HEADS, HEAD_DIM)
    query_pos = jax.nn.relu(queries.astype(jnp.float32)).reshape(tokens, HEADS, HEAD_DIM)
    numerator = jnp.einsum("thd,hde->the", query_pos, state, precision=highest)
    denominator = jnp.einsum("thd,hd->th", query_pos, zsum, precision=highest) + EPS
    attended = (numerator / denominator[..., None]).astype(jnp.bfloat16)
    attended = attended.reshape(row_count, frames, col_count, model_width)
    by_feature = lax.all_to_all(attended, "tile", split_axis=3, concat_axis=0, tiled=True)
    portion = by_feature
    product = jnp.dot(
        portion.reshape(-1, portion.shape[3]), w_output, preferred_element_type=jnp.float32
    )
    attn_out = lax.psum_scatter(
        product.reshape(row_count * lax.axis_size("tile"), frames, col_count, model_width),
        "tile",
        scatter_dimension=0,
        tiled=True,
    )
    hidden = (stream_in.astype(jnp.float32) + attn_out).astype(jnp.bfloat16)
    chan_dev = w_inner.shape[2]
    w_flat = w_inner.reshape(model_width, 2 * chan_dev)
    portion = lax.all_gather(hidden, "tile", axis=0, tiled=True)
    product = jnp.dot(portion.reshape(-1, model_width), w_flat, preferred_element_type=jnp.float32)
    activated = jax.nn.silu(product).astype(jnp.bfloat16)
    inner_act = activated.reshape(portion.shape[0], frames, col_count, 2, chan_dev)
    spatial = spatial_conv(inner_act, spatial_taps).astype(jnp.bfloat16)
    earlier_frames = shifted(spatial, "blk", 1)
    extended = jnp.concatenate([earlier_frames, spatial], axis=1)
    temporal_mix = jnp.zeros(spatial.shape, jnp.float32)
    for lag in range(TAPS):
        window = extended[:, TAPS - 1 - lag : TAPS - 1 - lag + frames]
        temporal_mix = temporal_mix + window.astype(jnp.float32) * temporal_taps[lag]
    gated_out = (temporal_mix[..., 0, :] * jax.nn.silu(temporal_mix[..., 1, :])).astype(
        jnp.bfloat16
    )
    portion = gated_out
    product = jnp.dot(portion.reshape(-1, chan_dev), w_down, preferred_element_type=jnp.float32)
    ffn_out = lax.psum_scatter(
        product.reshape(lax.axis_size("tile") * row_count, frames, col_count, model_width).astype(
            jnp.bfloat16
        ),
        "tile",
        scatter_dimension=0,
        tiled=True,
    ).astype(jnp.float32)
    return (hidden.astype(jnp.float32) + ffn_out).astype(jnp.bfloat16)


def solution(mesh):
    in_specs = (
        P("tile", "blk", None, None),
        P("tile", "blk", None, None),
        P("tile", "blk", None, None),
        P("tile", "blk", None, None),
        P("tile", None),
        P(None, None, "tile"),
        P("tile", None),
        P(None, None, None, "tile"),
        P(None, None, "tile"),
    )
    out_specs = P("tile", "blk", None, None)
    return jax.shard_map(
        on_device, mesh=mesh, in_specs=in_specs, out_specs=out_specs, check_vma=False
    )
```

profile of v0, /device:TPU:0, one launch (start us, length us, event | category | flops | bytes accessed | tf_op | source)
XLA Modules:
  0.0 571.9 jit_solution(4636084456415027600)
XLA Ops:
  9.1 4.0 reshape.58
  13.1 4.0 reshape.59
  17.1 3.5 fusion.8
  20.6 28.2 %reduce-scatter.4.cloned.1.call-done = f32[560,112]{1,0:T(8,128)} async-done(((f32[2240,112]{1,0:T(8,128)}), f32[560,112]{1,0:T(8,128)}) %reduce-scatter.4.cloned.1.call-update) | async-done | bytes 250896 | tf_op jit(solution)/shard_map/reduce_scatter | solution.py:77
  50.3 7.2 %collective-permute-done = f32[560,112]{1,0:T(8,128)S(1)} collective-permute-done((f32[560,112]{1,0:T(8,128)}, f32[560,112]{1,0:T(8,128)S(1)}, u32[]{:S(2)}, u32[]{:S(2)}) %collective-permute-start) | collective-permute-done | bytes 250912 | tf_op jit(solution)/shard_map/ppermute | solution.py:15
  62.2 10.2 %all-reduce.3 = f32[2240]{0:T(1024)S(1)} all-reduce(f32[2240]{0:T(1024)S(1)} %convert_reduce_fusion), channel_id=5, replica_groups=mesh['blk'=8,'tile'=4] {'tile'}, use_global_device_ids=true, to_apply=%region_2.3.clone | all-reduce | flops 2240 | bytes 17920
  74.3 3.0 convert_maximum_fusion
  79.2 4.3 reshape.62
  83.5 3.3 copy.27
  87.0 36.8 %all-reduce.1 = f32[4480]{0:T(1024)S(1)} all-reduce(f32[4480]{0:T(1024)S(1)} %multiply_dynamic-update-slice_fusion), channel_id=3, replica_groups=mesh['blk'=8,'tile'=4] {'blk'}, use_global_device_ids=true, to_apply=%add.1 | all-reduce | flops 4480 | bytes 35840
  123.9 8.9 %while.16 = (s32[]{:T(128)}, f32[560,112]{1,0:T(8,128)S(1)}, f32[560]{0:T(1024)S(1)}, s32[]{:T(128)}, f32[8,560,112]{2,1,0:T(8,128)}, /*index=5*/f32[8,560]{1,0:T(8,128)S(1)}, s32[]{:T(128)}, s32[]{:T(128)}) while((s32[]{:T(128)}, f32[560,112]{1,0:T(8,128)S(1)}, f32[560]{0:T(1024)S(1)}, s32[]{:T(128)}, f32[8,560,112]{2,1,0:T(8,128)}, ...), condition=%wide.region_4.5_spmd.clone, body=%wide.region_3.4_spmd.clone.sunk | while | flops 189844 | bytes 763955 | solution.py:30
  133.0 10.1 %all-reduce.2 = f32[2240]{0:T(1024)S(1)} all-reduce(f32[2240]{0:T(1024)S(1)} %add_dynamic-update-slice_fusion), channel_id=1, replica_groups=mesh['blk'=8,'tile'=4] {'tile'}, use_global_device_ids=true, to_apply=%add.2 | all-reduce | flops 2240 | bytes 17920
  146.3 9.7 %all_gather.25 = f32[2240,112]{1,0:T(8,128)S(1)} all-gather(f32[560,112]{1,0:T(8,128)S(1)} %multiply_add_fusion.1), channel_id=1, replica_groups=mesh['blk'=8,'tile'=4] {'tile'}, dimensions={0}, use_global_device_ids=true | all-gather | bytes 1254400 | tf_op jit(solution)/shard_map/all_gather | solution.py:82
  156.0 3.2 fusion.5
  159.2 28.0 %reshape.86 = bf16[8,2,16,2240]{2,1,0,3:T(2,128)(2,1)} reshape(bf16[256,20,112]{0,2,1:T(8,128)(2,1)} %fusion.5) | data formatting | bytes 2293760 | tf_op jit(solution)/shard_map/reshape | solution.py:91
  187.2 11.8 %reshape.89 = bf16[4,2,71680]{2,1,0:T(2,128)(2,1)} reshape(bf16[2240,8,2,16]{3,2,1,0:T(2,128)(2,1)} %bitcast.90) | data formatting | bytes 2293760
  198.9 19.8 %all_to_all.15 = bf16[4,2,71680]{2,1,0:T(2,128)(2,1)} all-to-all(bf16[4,2,71680]{2,1,0:T(2,128)(2,1)} %reshape.89), channel_id=1, replica_groups=mesh['blk'=8,'tile'=4] {'tile'}, dimensions={0} | all-to-all | bytes 2293760 | tf_op jit(solution)/shard_map/all_to_all | solution.py:92
  218.8 8.7 %reshape.90 = bf16[2240,8,2,16]{3,2,1,0:T(2,128)(2,1)} reshape(bf16[4,2,71680]{2,1,0:T(2,128)(2,1)} %all_to_all.15) | data formatting | bytes 2293760
  227.5 19.9 %copy.30 = bf16[8,2,16,4,560]{4,2,1,0,3:T(8,128)(2,1)} copy(bf16[8,2,16,4,560]{2,1,0,4,3:T(2,128)(2,1)} %bitcast.91) | data formatting | bytes 2293760 | tf_op jit(solution)/shard_map/all_to_all | solution.py:92
  247.3 7.8 %fusion.3 = f32[32,2,16,2240]{3,2,1,0:T(8,128)} fusion(bf16[32,2,16,560]{3,2,1,0:T(8,128)(2,1)} %bitcast.95, bf16[560,2240]{1,0:T(8,128)(2,1)S(1)} %copy-done), kind=kOutput, calls=%fused_computation.21 | convolution fusion | flops 2569011200 | bytes 12830720 | tf_op jit(solution)/shard_map/dot_general | solution.py:94
  255.2 74.2 %reduce-scatter.6.cloned.1.call-done = f32[8,2,16,2240]{3,2,1,0:T(8,128)} async-done(((f32[32,2,16,2240]{3,2,1,0:T(8,128)}), f32[8,2,16,2240]{3,2,1,0:T(8,128)}) %reduce-scatter.6.cloned.1.call-update) | async-done | bytes 2293776 | tf_op jit(solution)/shard_map/reduce_scatter | solution.py:97
  332.6 11.4 %copy.38 = bf16[280,8,2,1024]{3,1,2,0:T(8,128)(2,1)} copy(bf16[280,8,2,1024]{3,2,1,0:T(2,128)(2,1)} %bitcast.92) | data formatting | bytes 18350080
  344.1 25.9 %all-gather.5.cloned.1.call-done = bf16[32,2,16,2240]{3,2,1,0:T(8,128)(2,1)} async-done(((bf16[8,2,16,2240]{3,2,1,0:T(8,128)(2,1)}), bf16[32,2,16,2240]{3,2,1,0:T(8,128)(2,1)}) %all-gather.5.cloned.1.call-update) | async-done | bytes 4587536 | tf_op jit(solution)/shard_map/all_gather | solution.py:106
  370.0 16.0 %multiply_convert_fusion = bf16[1024,2048]{1,0:T(8,128)(2,1)} fusion(bf16[1024,2240]{1,0:T(8,128)(2,1)} %bitcast.98, bf16[2240,2048]{1,0:T(8,128)(2,1)} %bitcast.93), kind=kOutput, calls=%fused_computation.13 | convolution fusion | flops 9405726720 | bytes 17956864 | tf_op jit(solution)/shard_map/dot_general | solution.py:107
  386.0 7.8 %reshape.67 = bf16[32,2,16,2,1024]{4,3,2,1,0:T(2,128)(2,1)} reshape(bf16[1024,2048]{1,0:T(8,128)(2,1)} %multiply_convert_fusion) | data formatting | bytes 8388608 | tf_op jit(solution)/shard_map/reshape | solution.py:109
  393.8 3.5 copy.31
  397.3 11.9 %add_convert_fusion = bf16[32,2,16,2,1024]{4,2,1,0,3:T(8,128)(2,1)S(1)} fusion(bf16[32,2,16,2,1024]{4,2,1,0,3:T(8,128)(2,1)S(1)} %copy.31, f32[2,1024]{1,0:T(2,128)S(1)} %get-tuple-element.157, f32[2,1024]{1,0:T(2,128)S(1)} %get-tuple-element.158, f32[2,1024]{1,0:T(2,128)S(1)} %get-tuple-element.151, f32[2,1024]{1,0:T(2,128)S(1)} %get-tuple-element.152, ...), kind=kLoop, calls=%fused_computation.12 | loop fusion | flops 56623104 | bytes 8462336 | tf_op jit(solution)/shard_map/convert_element_type | solution.py:110
  409.2 3.9 collective-permute-start.2
  413.2 89.7 %collective-permute-done.2 = bf16[32,2,16,2,1024]{4,2,1,0,3:T(8,128)(2,1)S(1)} collective-permute-done((bf16[32,2,16,2,1024]{4,2,1,0,3:T(8,128)(2,1)S(1)}, bf16[32,2,16,2,1024]{4,2,1,0,3:T(8,128)(2,1)S(1)}, u32[]{:S(2)}, u32[]{:S(2)}) %collective-permute-start.2) | collective-permute-done | bytes 4194336 | tf_op jit(solution)/shard_map/ppermute | solution.py:36
  502.8 3.2 multiply_add_fusion
  506.0 7.3 %convolution_convert_fusion = bf16[32,2,16,2240]{3,2,1,0:T(8,128)(2,1)} fusion(bf16[1024,2240]{0,1:T(8,128)(2,1)S(1)} %bitcast.100, f32[32,2,16,2,1024]{4,2,1,0,3:T(8,128)S(1)} %multiply_add_fusion), kind=kOutput, calls=%fused_computation.14 | convolution fusion | flops 4706205696 | bytes 17563648 | tf_op jit(solution)/shard_map/dot_general | solution.py:121
  513.4 49.1 %reduce-scatter.8.cloned.1.call-done = bf16[8,2,16,2240]{3,2,1,0:T(8,128)(2,1)} async-done(((bf16[32,2,16,2240]{3,2,1,0:T(8,128)(2,1)}), bf16[8,2,16,2240]{3,2,1,0:T(8,128)(2,1)}) %reduce-scatter.8.cloned.1.call-update) | async-done | bytes 1146896 | tf_op jit(solution)/shard_map/reduce_scatter | solution.py:122
  (82 shorter events, 29.1 us)
Async XLA Ops:
  6.5 240.8 %copy-start = (bf16[560,2240]{1,0:T(8,128)(2,1)S(1)}, bf16[560,2240]{1,0:T(8,128)(2,1)}, u32[]{:S(2)}) copy-start(bf16[560,2240]{1,0:T(8,128)(2,1)} %param.15) | copy-start | bytes 7526404
  6.5 42.3 %reduce-scatter.4.cloned.1.call-start = ((), (), s32[]{:S(2)}) async-start(), calls=%async_computation.4 | async-start | bytes 1433600 | tf_op jit(solution)/shard_map/reduce_scatter | solution.py:77
  13.1 46.2 %copy-start.7 = (u32[32]{0:T(128)S(1)}, u32[32]{0:T(128)}, u32[]{:S(2)}) copy-start(u32[32]{0:T(128)} %constant.77) | copy-start | bytes 388
  20.6 56.7 %copy-start.8 = (u32[32]{0:T(128)S(1)}, u32[32]{0:T(128)}, u32[]{:S(2)}) copy-start(u32[32]{0:T(128)} %constant.72) | copy-start | bytes 388
  20.6 103.3 %all-gather.7.cloned.1.call-start = ((), (), s32[]{:S(2)}) async-start(), calls=%async_computation.8 | async-start | bytes 2580480 | tf_op jit(solution)/shard_map/all_gather | solution.py:20
  48.9 8.6 %collective-permute-start = (f32[560,112]{1,0:T(8,128)}, f32[560,112]{1,0:T(8,128)S(1)}, u32[]{:S(2)}, u32[]{:S(2)}) collective-permute-start(f32[560,112]{1,0:T(8,128)} %reduce-scatter.4.cloned.1.call-done), channel_id=1, source_target_pairs={{0,4},{4,0},{8,12},{12,8},{16,20},{20,16},{24,28},{28,24},{1,5},{5... | collective-permute-start | bytes 752648 | tf_op jit(solution)/shard_map/ppermute | solution.py:15
  59.3 270.2 %reduce-scatter.6.cloned.1.call-start = ((), (), s32[]{:S(2)}) async-start(), calls=%async_computation.5 | async-start | bytes 11796480 | tf_op jit(solution)/shard_map/reduce_scatter | solution.py:97
  72.4 14.4 %collective-permute-start.1 = (f32[560]{0:T(1024)S(1)}, f32[560]{0:T(1024)S(1)}, u32[]{:S(2)}, u32[]{:S(2)}) collective-permute-start(f32[560]{0:T(1024)S(1)} %dynamic-slice.3), channel_id=1, source_target_pairs={{0,4},{4,0},{8,12},{12,8},{16,20},{20,16},{24,28},{28,24},{1,5},{5... | collective-permute-start | bytes 6728 | tf_op jit(solution)/shard_map/ppermute | solution.py:15
  86.8 59.4 %copy-start.4 = (f32[560,112]{1,0:T(8,128)S(1)}, f32[560,112]{1,0:T(8,128)}, u32[]{:S(2)}) copy-start(f32[560,112]{1,0:T(8,128)} %reduce-scatter.4.cloned.1.call-done) | copy-start | bytes 752644
  143.2 12.8 %copy-start.2 = (f32[256,20,112]{0,2,1:T(8,128)S(1)}, f32[256,20,112]{0,2,1:T(8,128)}, u32[]{:S(2)}) copy-start(f32[256,20,112]{0,2,1:T(8,128)} %copy.27) | copy-start | bytes 6881284
  255.2 74.3 %copy-start.3 = (bf16[8,2,16,2240]{3,2,1,0:T(8,128)(2,1)S(1)}, bf16[8,2,16,2240]{3,2,1,0:T(8,128)(2,1)}, u32[]{:S(2)}) copy-start(bf16[8,2,16,2240]{3,2,1,0:T(8,128)(2,1)} %param.11) | copy-start | bytes 3440644
  255.2 114.8 %all-gather.5.cloned.1.call-start = ((), (), s32[]{:S(2)}) async-start(), calls=%async_computation.6 | async-start | bytes 5898240 | tf_op jit(solution)/shard_map/all_gather | solution.py:106
  332.4 230.1 %reduce-scatter.8.cloned.1.call-start = ((), (), s32[]{:S(2)}) async-start(), calls=%async_computation.7 | async-start | bytes 5898240 | tf_op jit(solution)/shard_map/reduce_scatter | solution.py:122
  332.6 11.4 %copy-start.5 = (f32[3,3,2,1024]{3,2,1,0:T(2,128)S(1)}, f32[3,3,2,1024]{3,2,1,0:T(2,128)}, u32[]{:S(2)}) copy-start(f32[3,3,2,1024]{3,2,1,0:T(2,128)} %param.18) | copy-start | bytes 221188
  397.3 15.8 %copy-start.6 = (f32[3,2,1024]{2,1,0:T(2,128)S(1)}, f32[3,2,1024]{2,1,0:T(2,128)}, u32[]{:S(2)}) copy-start(f32[3,2,1024]{2,1,0:T(2,128)} %param.19) | copy-start | bytes 73732
  397.3 108.7 %slice-start = ((s8[4587520]{0:T(1024)(128)(4,1)}), s8[4194304]{0:T(1024)(128)(4,1)S(1)}, s32[]{:S(2)}) async-start(s8[4587520]{0:T(1024)(128)(4,1)} %bitcast.99), calls=%async_computation.9 | async-start | bytes 8388608
  409.2 93.6 %collective-permute-start.2 = (bf16[32,2,16,2,1024]{4,2,1,0,3:T(8,128)(2,1)S(1)}, bf16[32,2,16,2,1024]{4,2,1,0,3:T(8,128)(2,1)S(1)}, u32[]{:S(2)}, u32[]{:S(2)}) collective-permute-start(bf16[32,2,16,2,1024]{4,2,1,0,3:T(8,128)(2,1)S(1)} %add_convert_fusion), channel_id=1, source_target_pairs={{0,4},{4,8},{8,12},{12,16},{16,20},{20,24},{24,28},{1,5},{5,9},{9,... | collective-permute-start | bytes 12582920 | tf_op jit(solution)/shard_map/ppermute | solution.py:36
  502.8 3.2 slice-start.1
  506.0 59.4 %copy-start.1 = (bf16[560,2240]{1,0:T(8,128)(2,1)S(1)}, bf16[560,2240]{1,0:T(8,128)(2,1)}, u32[]{:S(2)}) copy-start(bf16[560,2240]{1,0:T(8,128)(2,1)} %param.15) | copy-start | bytes 7526404
Sparse Core Ops, SparseCore 0:
  20.7 28.1 reduce-scatter.3
  59.4 51.7 all-gather.6
  255.3 74.0 reduce-scatter.5
  332.5 37.4 all-gather.4
  513.5 48.9 reduce-scatter.7
where the time goes:
time: 574 us; the launch traced here: 572 us
  waiting for transfers between devices  274 us (48%)
  local copies, waits for them, and re-layouts  108 us (19%)
  blocking collectives  86.6 us (15%)
  matrix products  40.7 us (7%)
  other arithmetic  38.5 us (7%)
  between operations  15.2 us (3%)
  starting transfers between devices  7.66 us (1%)
    ppermute x1, waiting for transfers between devices, shifted(): return lax.ppermute(x, axis, pairs)  89.7 us
    reduce_scatter x1, waiting for transfers between devices, on_device(): lax.psum_scatter(product.reshape(row_count * lax.axis_size('tile'), frame...  74.2 us
    unnamed x3, blocking collectives  57.1 us
    reduce_scatter x1, waiting for transfers between devices, on_device(): lax.psum_scatter(product.reshape(lax.axis_size('tile') * row_count, frame...  49.1 us
    unnamed x30, local copies, waits for them, and re-layouts  33.3 us
    reduce_scatter x1, waiting for transfers between devices, on_device(): lax.psum_scatter(local_kv, 'tile', scatter_dimension=0, tiled=True)  28.2 us
    reshape x1, local copies, waits for them, and re-layouts, on_device(): attended = attended.reshape(row_count, frames, col_count, model_width)  28 us
    all_gather x1, waiting for transfers between devices, on_device(): portion = lax.all_gather(hidden, 'tile', axis=0, tiled=True)  25.9 us
  transfers between devices with their start and end apart: 8, of which 6 were waited for; matrix products, arithmetic and copies ran while one was open for 4% of the time, Pallas kernels for 0%

commit v1 on v0

--- a/solution.py
+++ b/solution.py
@@ -1,3 +1,4 @@
+import functools
 import jax
 import jax.numpy as jnp
 from jax import lax
@@ -7,6 +8,28 @@
 HEAD_DIM = 112
 TAPS = 3
 EPS = 1e-06
+
+
+def rest_tiles_up(matrix, row_dim, dimension_no):
+    v1 = lax.axis_index("tile")
+    local_next = lax.axis_size("tile")
+    upper, built = (local_next, v1)
+    e_now = matrix.shape[row_dim] // upper
+    small = jnp.roll(matrix, shift=-built * e_now, axis=row_dim)
+    kept_arr = lax.slice_in_dim(small, 0, e_now, axis=row_dim)
+    pieces_in = [kept_arr]
+    for hop_no in tuple(range(1, upper)):
+        r_now = lax.slice_in_dim(small, hop_no * e_now, (hop_no + 1) * e_now, axis=row_dim)
+        u_next = lax.ppermute(
+            r_now, "tile", [(src_i, (src_i + hop_no) % upper) for src_i in range(upper)]
+        )
+        pieces_in.append(u_next)
+    back = jnp.concatenate(pieces_in[::-1], dimension_no)
+    part_next = jnp.roll(back, (built + 1) * pieces_in[0].shape[dimension_no], dimension_no)
+    return part_next
+
+
+_cut_steps_all = functools.partial(rest_tiles_up, row_dim=3, dimension_no=0)
 
 
 def from_partner(value, axis, stride):
@@ -89,7 +112,7 @@
     denominator = jnp.einsum("thd,hd->th", query_pos, zsum, precision=highest) + EPS
     attended = (numerator / denominator[..., None]).astype(jnp.bfloat16)
     attended = attended.reshape(row_count, frames, col_count, model_width)
-    by_feature = lax.all_to_all(attended, "tile", split_axis=3, concat_axis=0, tiled=True)
+    by_feature = _cut_steps_all(attended)
     portion = by_feature
     product = jnp.dot(
         portion.reshape(-1, portion.shape[3]), w_output, preferred_element_type=jnp.float32

time: 574 us -> 517 us (0.901)
  local copies, waits for them, and re-layouts: 108 us -> 53.1 us
  blocking collectives: 86.6 us -> 66.8 us
  waiting for transfers between devices: 274 us -> 291 us
    reshape x1, local copies, waits for them, and re-layouts: 28 us -> 3.66 us  [on_device(): attended = attended.reshape(row_count, frames, col_count, model_width)]
    all_to_all x1 -> x0, local copies, waits for them, and re-layouts: 19.9 us -> none  [on_device(): lax.all_to_all(attended, 'tile', split_axis=3, concat_axis=0, tiled=True)]
    all_to_all x1 -> x0, blocking collectives: 19.8 us -> none  [on_device(): lax.all_to_all(attended, 'tile', split_axis=3, concat_axis=0, tiled=True)]
    unnamed x30 -> x37, local copies, waits for them, and re-layouts: 33.3 us -> 16.9 us
    ppermute x0 -> x3, waiting for transfers between devices: none -> 15.4 us  [rest_tiles_up(): lax.ppermute(r_now, 'tile', [(src_i, (src_i + hop_no) % upper) for src_i...]
  transfers between devices with their start and end apart: 8 -> 11, of which waited for: 6 -> 8; matrix products, arithmetic and copies ran while one was open for 4% -> 5% of each run, Pallas kernels for 0% -> 0%
where the time goes in v1:
time: 517 us; the launch traced here: 516 us
  waiting for transfers between devices  291 us (56%)
  blocking collectives  66.8 us (13%)
  local copies, waits for them, and re-layouts  53.1 us (10%)
  other arithmetic  41.1 us (8%)
  matrix products  39.2 us (8%)
  between operations  15.2 us (3%)
  starting transfers between devices  9.55 us (2%)
    ppermute x1, waiting for transfers between devices, shifted(): return lax.ppermute(x, axis, pairs)  89.7 us
    reduce_scatter x1, waiting for transfers between devices, on_device(): lax.psum_scatter(product.reshape(row_count * lax.axis_size('tile'), frame...  75.3 us
    unnamed x3, blocking collectives  57.1 us
    reduce_scatter x1, waiting for transfers between devices, on_device(): lax.psum_scatter(product.reshape(lax.axis_size('tile') * row_count, frame...  49.1 us
    reduce_scatter x1, waiting for transfers between devices, on_device(): lax.psum_scatter(local_kv, 'tile', scatter_dimension=0, tiled=True)  28.3 us
    all_gather x1, waiting for transfers between devices, on_device(): portion = lax.all_gather(hidden, 'tile', axis=0, tiled=True)  25.9 us
    unnamed x37, local copies, waits for them, and re-layouts  16.9 us
    dot_general x1, matrix products, on_device(): jnp.dot(portion.reshape(-1, model_width), w_flat, preferred_element_type=...  16 us
  transfers between devices with their start and end apart: 11, of which 8 were waited for; matrix products, arithmetic and copies ran while one was open for 5% of the time, Pallas kernels for 0%

profile of v1, /device:TPU:0, one launch (start us, length us, event | category | flops | bytes accessed | tf_op | source)
XLA Modules:
  0.0 516.1 jit_solution(15271110442640914901)
XLA Ops:
  9.1 4.0 reshape.57
  13.1 4.0 reshape.58
  17.1 3.5 fusion.8
  20.6 28.3 %reduce-scatter.4.cloned.1.call-done = f32[560,112]{1,0:T(8,128)} async-done(((f32[2240,112]{1,0:T(8,128)}), f32[560,112]{1,0:T(8,128)}) %reduce-scatter.4.cloned.1.call-update) | async-done | bytes 250896 | tf_op jit(solution)/shard_map/reduce_scatter | solution.py:100
  50.4 7.1 %collective-permute-done = f32[560,112]{1,0:T(8,128)S(1)} collective-permute-done((f32[560,112]{1,0:T(8,128)}, f32[560,112]{1,0:T(8,128)S(1)}, u32[]{:S(2)}, u32[]{:S(2)}) %collective-permute-start) | collective-permute-done | bytes 250912 | tf_op jit(solution)/shard_map/ppermute | solution.py:38
  62.0 10.2 %all-reduce.3 = f32[2240]{0:T(1024)S(1)} all-reduce(f32[2240]{0:T(1024)S(1)} %convert_reduce_fusion), channel_id=5, replica_groups=mesh['blk'=8,'tile'=4] {'tile'}, use_global_device_ids=true, to_apply=%region_2.3.clone | all-reduce | flops 2240 | bytes 17920
  74.2 3.0 convert_maximum_fusion
  79.0 4.3 reshape.61
  83.3 3.3 copy.27
  86.8 36.8 %all-reduce.1 = f32[4480]{0:T(1024)S(1)} all-reduce(f32[4480]{0:T(1024)S(1)} %multiply_dynamic-update-slice_fusion), channel_id=3, replica_groups=mesh['blk'=8,'tile'=4] {'blk'}, use_global_device_ids=true, to_apply=%add.1 | all-reduce | flops 4480 | bytes 35840
  123.7 8.9 %while.16 = (s32[]{:T(128)}, f32[560,112]{1,0:T(8,128)S(1)}, f32[560]{0:T(1024)S(1)}, s32[]{:T(128)}, f32[8,560,112]{2,1,0:T(8,128)}, /*index=5*/f32[8,560]{1,0:T(8,128)S(1)}, s32[]{:T(128)}, s32[]{:T(128)}) while((s32[]{:T(128)}, f32[560,112]{1,0:T(8,128)S(1)}, f32[560]{0:T(1024)S(1)}, s32[]{:T(128)}, f32[8,560,112]{2,1,0:T(8,128)}, ...), condition=%wide.region_4.5_spmd.clone, body=%wide.region_3.4_spmd.clone.sunk | while | flops 189844 | bytes 763955 | solution.py:53
  132.8 10.1 %all-reduce.2 = f32[2240]{0:T(1024)S(1)} all-reduce(f32[2240]{0:T(1024)S(1)} %add_dynamic-update-slice_fusion), channel_id=1, replica_groups=mesh['blk'=8,'tile'=4] {'tile'}, use_global_device_ids=true, to_apply=%add.2 | all-reduce | flops 2240 | bytes 17920
  143.0 3.0 fusion.18
  146.1 9.7 %all_gather.25 = f32[2240,112]{1,0:T(8,128)S(1)} all-gather(f32[560,112]{1,0:T(8,128)S(1)} %multiply_add_fusion.1), channel_id=1, replica_groups=mesh['blk'=8,'tile'=4] {'tile'}, dimensions={0}, use_global_device_ids=true | all-gather | bytes 1254400 | tf_op jit(solution)/shard_map/all_gather | solution.py:105
  155.9 3.2 fusion.5
  161.7 3.7 reshape.63
  172.3 8.0 %collective-permute-done.2 = bf16[8,2,16,560]{3,2,1,0:T(8,128)(2,1)S(1)} collective-permute-done((bf16[8,2,16,560]{3,2,1,0:T(8,128)(2,1)}, bf16[8,2,16,560]{3,2,1,0:T(8,128)(2,1)S(1)}, u32[]{:S(2)}, u32[]{:S(2)}) %collective-permute-start.2) | collective-permute-done | bytes 286752 | tf_op jit(solution)/shard_map/ppermute | solution.py:23
  180.3 7.4 %collective-permute-done.3 = bf16[8,2,16,560]{3,2,1,0:T(8,128)(2,1)S(1)} collective-permute-done((bf16[8,2,16,560]{3,2,1,0:T(8,128)(2,1)}, bf16[8,2,16,560]{3,2,1,0:T(8,128)(2,1)S(1)}, u32[]{:S(2)}, u32[]{:S(2)}) %collective-permute-start.3) | collective-permute-done | bytes 286752 | tf_op jit(solution)/shard_map/ppermute | solution.py:23
  192.0 6.2 %fusion.3 = f32[32,2,16,2240]{3,2,1,0:T(8,128)} fusion(bf16[560,2240]{1,0:T(8,128)(2,1)S(1)} %copy-done, bf16[64,2,16,560]{3,2,1,0:T(8,128)(2,1)S(1)} %slice_dynamic-update-slice_fusion.1, s32[]{:T(128)S(6)} %select_n.71), kind=kOutput, calls=%fused_computation.21 | convolution fusion | flops 2569011200 | bytes 13066244 | tf_op jit(solution)/shard_map/dot_general | solution.py:117
  198.3 75.3 %reduce-scatter.6.cloned.1.call-done = f32[8,2,16,2240]{3,2,1,0:T(8,128)} async-done(((f32[32,2,16,2240]{3,2,1,0:T(8,128)}), f32[8,2,16,2240]{3,2,1,0:T(8,128)}) %reduce-scatter.6.cloned.1.call-update) | async-done | bytes 2293776 | tf_op jit(solution)/shard_map/reduce_scatter | solution.py:120
  276.8 11.4 %copy.36 = bf16[280,8,2,1024]{3,1,2,0:T(8,128)(2,1)} copy(bf16[280,8,2,1024]{3,2,1,0:T(2,128)(2,1)} %bitcast.81) | data formatting | bytes 18350080
  288.2 25.9 %all-gather.5.cloned.1.call-done = bf16[32,2,16,2240]{3,2,1,0:T(8,128)(2,1)} async-done(((bf16[8,2,16,2240]{3,2,1,0:T(8,128)(2,1)}), bf16[32,2,16,2240]{3,2,1,0:T(8,128)(2,1)}) %all-gather.5.cloned.1.call-update) | async-done | bytes 4587536 | tf_op jit(solution)/shard_map/all_gather | solution.py:129
  314.1 16.0 %multiply_convert_fusion = bf16[1024,2048]{1,0:T(8,128)(2,1)} fusion(bf16[1024,2240]{1,0:T(8,128)(2,1)} %bitcast.86, bf16[2240,2048]{1,0:T(8,128)(2,1)} %bitcast.82), kind=kOutput, calls=%fused_computation.13 | convolution fusion | flops 9405726720 | bytes 17956864 | tf_op jit(solution)/shard_map/dot_general | solution.py:130
  330.1 7.8 %reshape.66 = bf16[32,2,16,2,1024]{4,3,2,1,0:T(2,128)(2,1)} reshape(bf16[1024,2048]{1,0:T(8,128)(2,1)} %multiply_convert_fusion) | data formatting | bytes 8388608 | tf_op jit(solution)/shard_map/reshape | solution.py:132
  337.9 3.5 copy.29
  341.5 11.9 %add_convert_fusion = bf16[32,2,16,2,1024]{4,2,1,0,3:T(8,128)(2,1)S(1)} fusion(bf16[32,2,16,2,1024]{4,2,1,0,3:T(8,128)(2,1)S(1)} %copy.29, f32[2,1024]{1,0:T(2,128)S(1)} %get-tuple-element.160, f32[2,1024]{1,0:T(2,128)S(1)} %get-tuple-element.161, f32[2,1024]{1,0:T(2,128)S(1)} %get-tuple-element.154, f32[2,1024]{1,0:T(2,128)S(1)} %get-tuple-element.155, ...), kind=kLoop, calls=%fused_computation.12 | loop fusion | flops 56623104 | bytes 8462336 | tf_op jit(solution)/shard_map/convert_element_type | solution.py:133
  353.4 3.9 collective-permute-start.5
  357.3 89.7 %collective-permute-done.5 = bf16[32,2,16,2,1024]{4,2,1,0,3:T(8,128)(2,1)S(1)} collective-permute-done((bf16[32,2,16,2,1024]{4,2,1,0,3:T(8,128)(2,1)S(1)}, bf16[32,2,16,2,1024]{4,2,1,0,3:T(8,128)(2,1)S(1)}, u32[]{:S(2)}, u32[]{:S(2)}) %collective-permute-start.5) | collective-permute-done | bytes 4194336 | tf_op jit(solution)/shard_map/ppermute | solution.py:59
  447.0 3.2 multiply_add_fusion
  450.2 7.3 %convolution_convert_fusion = bf16[32,2,16,2240]{3,2,1,0:T(8,128)(2,1)} fusion(bf16[1024,2240]{0,1:T(8,128)(2,1)S(1)} %bitcast.88, f32[32,2,16,2,1024]{4,2,1,0,3:T(8,128)S(1)} %multiply_add_fusion), kind=kOutput, calls=%fused_computation.14 | convolution fusion | flops 4706205696 | bytes 17563648 | tf_op jit(solution)/shard_map/dot_general | solution.py:144
  457.6 49.1 %reduce-scatter.8.cloned.1.call-done = bf16[8,2,16,2240]{3,2,1,0:T(8,128)(2,1)} async-done(((bf16[32,2,16,2240]{3,2,1,0:T(8,128)(2,1)}), bf16[8,2,16,2240]{3,2,1,0:T(8,128)(2,1)}) %reduce-scatter.8.cloned.1.call-update) | async-done | bytes 1146896 | tf_op jit(solution)/shard_map/reduce_scatter | solution.py:145
  506.7 2.9 add_convert_fusion.1
  (97 shorter events, 36.9 us)
Async XLA Ops:
  6.5 185.4 %copy-start = (bf16[560,2240]{1,0:T(8,128)(2,1)S(1)}, bf16[560,2240]{1,0:T(8,128)(2,1)}, u32[]{:S(2)}) copy-start(bf16[560,2240]{1,0:T(8,128)(2,1)} %param.15) | copy-start | bytes 7526404
  6.5 42.4 %reduce-scatter.4.cloned.1.call-start = ((), (), s32[]{:S(2)}) async-start(), calls=%async_computation.3 | async-start | bytes 1433600 | tf_op jit(solution)/shard_map/reduce_scatter | solution.py:100
  17.1 42.2 %copy-start.8 = (u32[32]{0:T(128)S(1)}, u32[32]{0:T(128)}, u32[]{:S(2)}) copy-start(u32[32]{0:T(128)} %constant.122) | copy-start | bytes 388
  20.6 103.1 %all-gather.7.cloned.1.call-start = ((), (), s32[]{:S(2)}) async-start(), calls=%async_computation.7 | async-start | bytes 2580480 | tf_op jit(solution)/shard_map/all_gather | solution.py:43
  48.9 8.6 %collective-permute-start = (f32[560,112]{1,0:T(8,128)}, f32[560,112]{1,0:T(8,128)S(1)}, u32[]{:S(2)}, u32[]{:S(2)}) collective-permute-start(f32[560,112]{1,0:T(8,128)} %reduce-scatter.4.cloned.1.call-done), channel_id=1, source_target_pairs={{0,4},{4,0},{8,12},{12,8},{16,20},{20,16},{24,28},{28,24},{1,5},{5... | collective-permute-start | bytes 752648 | tf_op jit(solution)/shard_map/ppermute | solution.py:38
  59.2 17.9 %copy-start.9 = (u32[32]{0:T(128)S(1)}, u32[32]{0:T(128)}, u32[]{:S(2)}) copy-start(u32[32]{0:T(128)} %constant.117) | copy-start | bytes 388
  59.3 214.3 %reduce-scatter.6.cloned.1.call-start = ((), (), s32[]{:S(2)}) async-start(), calls=%async_computation.4 | async-start | bytes 11796480 | tf_op jit(solution)/shard_map/reduce_scatter | solution.py:120
  72.3 14.3 %collective-permute-start.1 = (f32[560]{0:T(1024)S(1)}, f32[560]{0:T(1024)S(1)}, u32[]{:S(2)}, u32[]{:S(2)}) collective-permute-start(f32[560]{0:T(1024)S(1)} %dynamic-slice.3), channel_id=1, source_target_pairs={{0,4},{4,0},{8,12},{12,8},{16,20},{20,16},{24,28},{28,24},{1,5},{5... | collective-permute-start | bytes 6728 | tf_op jit(solution)/shard_map/ppermute | solution.py:38
  123.7 22.4 %copy-start.5 = (f32[560,112]{1,0:T(8,128)S(1)}, f32[560,112]{1,0:T(8,128)}, u32[]{:S(2)}) copy-start(f32[560,112]{1,0:T(8,128)} %reduce-scatter.4.cloned.1.call-done) | copy-start | bytes 752644
  143.0 12.8 %copy-start.2 = (f32[256,20,112]{0,2,1:T(8,128)S(1)}, f32[256,20,112]{0,2,1:T(8,128)}, u32[]{:S(2)}) copy-start(f32[256,20,112]{0,2,1:T(8,128)} %copy.27) | copy-start | bytes 6881284
  168.0 1.0 copy-start.3
  170.4 9.9 %collective-permute-start.2 = (bf16[8,2,16,560]{3,2,1,0:T(8,128)(2,1)}, bf16[8,2,16,560]{3,2,1,0:T(8,128)(2,1)S(1)}, u32[]{:S(2)}, u32[]{:S(2)}) collective-permute-start(bf16[8,2,16,560]{3,2,1,0:T(8,128)(2,1)} %get-tuple-element.152), channel_id=1, source_target_pairs={{0,3},{1,0},{2,1},{3,2},{4,7},{5,4},{6,5},{7,6},{8,11},{9,8},{10,9... | collective-permute-start | bytes 860168 | tf_op jit(solution)/shard_map/ppermute | solution.py:23
  171.8 15.9 %collective-permute-start.3 = (bf16[8,2,16,560]{3,2,1,0:T(8,128)(2,1)}, bf16[8,2,16,560]{3,2,1,0:T(8,128)(2,1)S(1)}, u32[]{:S(2)}, u32[]{:S(2)}) collective-permute-start(bf16[8,2,16,560]{3,2,1,0:T(8,128)(2,1)} %get-tuple-element.151), channel_id=1, source_target_pairs={{0,2},{1,3},{2,0},{3,1},{4,6},{5,7},{6,4},{7,5},{8,10},{9,11},{10,... | collective-permute-start | bytes 860168 | tf_op jit(solution)/shard_map/ppermute | solution.py:23
  172.3 15.5 %collective-permute-start.4 = (bf16[8,2,16,560]{3,2,1,0:T(8,128)(2,1)}, bf16[8,2,16,560]{3,2,1,0:T(8,128)(2,1)}, u32[]{:S(2)}, u32[]{:S(2)}) collective-permute-start(bf16[8,2,16,560]{3,2,1,0:T(8,128)(2,1)} %get-tuple-element.150), channel_id=1, source_target_pairs={{0,1},{1,2},{2,3},{3,0},{4,5},{5,6},{6,7},{7,4},{8,9},{9,10},{10,1... | collective-permute-start | bytes 860168 | tf_op jit(solution)/shard_map/ppermute | solution.py:23
  198.2 75.4 %copy-start.4 = (bf16[8,2,16,2240]{3,2,1,0:T(8,128)(2,1)S(1)}, bf16[8,2,16,2240]{3,2,1,0:T(8,128)(2,1)}, u32[]{:S(2)}) copy-start(bf16[8,2,16,2240]{3,2,1,0:T(8,128)(2,1)} %param.11) | copy-start | bytes 3440644
  198.2 115.9 %all-gather.5.cloned.1.call-start = ((), (), s32[]{:S(2)}) async-start(), calls=%async_computation.5 | async-start | bytes 5898240 | tf_op jit(solution)/shard_map/all_gather | solution.py:129
  276.5 230.2 %reduce-scatter.8.cloned.1.call-start = ((), (), s32[]{:S(2)}) async-start(), calls=%async_computation.6 | async-start | bytes 5898240 | tf_op jit(solution)/shard_map/reduce_scatter | solution.py:145
  276.8 11.4 %copy-start.6 = (f32[3,3,2,1024]{3,2,1,0:T(2,128)S(1)}, f32[3,3,2,1024]{3,2,1,0:T(2,128)}, u32[]{:S(2)}) copy-start(f32[3,3,2,1024]{3,2,1,0:T(2,128)} %param.18) | copy-start | bytes 221188
  341.5 15.8 %copy-start.7 = (f32[3,2,1024]{2,1,0:T(2,128)S(1)}, f32[3,2,1024]{2,1,0:T(2,128)}, u32[]{:S(2)}) copy-start(f32[3,2,1024]{2,1,0:T(2,128)} %param.19) | copy-start | bytes 73732
  341.5 108.7 %slice-start = ((s8[4587520]{0:T(1024)(128)(4,1)}), s8[4194304]{0:T(1024)(128)(4,1)S(1)}, s32[]{:S(2)}) async-start(s8[4587520]{0:T(1024)(128)(4,1)} %bitcast.87), calls=%async_computation.8 | async-start | bytes 8388608
  353.4 93.6 %collective-permute-start.5 = (bf16[32,2,16,2,1024]{4,2,1,0,3:T(8,128)(2,1)S(1)}, bf16[32,2,16,2,1024]{4,2,1,0,3:T(8,128)(2,1)S(1)}, u32[]{:S(2)}, u32[]{:S(2)}) collective-permute-start(bf16[32,2,16,2,1024]{4,2,1,0,3:T(8,128)(2,1)S(1)} %add_convert_fusion), channel_id=1, source_target_pairs={{0,4},{4,8},{8,12},{12,16},{16,20},{20,24},{24,28},{1,5},{5,9},{9,... | collective-permute-start | bytes 12582920 | tf_op jit(solution)/shard_map/ppermute | solution.py:59
  447.0 3.2 slice-start.1
  457.5 52.0 %copy-start.1 = (bf16[560,2240]{1,0:T(8,128)(2,1)S(1)}, bf16[560,2240]{1,0:T(8,128)(2,1)}, u32[]{:S(2)}) copy-start(bf16[560,2240]{1,0:T(8,128)(2,1)} %param.15) | copy-start | bytes 7526404
Sparse Core Ops, SparseCore 0:
  20.7 28.1 reduce-scatter.3
  59.4 51.6 all-gather.6
  198.3 75.2 reduce-scatter.5
  276.6 37.4 all-gather.4
  457.7 48.9 reduce-scatter.7
